TPU v7x, 32 devices: a whole 2x2x4 slice. The times are simulated.
32 devices in a mesh: pts: 8 (over z, y), grp: 4 (over x, core).
Axes of the slice: x: 2, y: 2, z: 4, core: 2. Of those that a mesh axis runs over, the one named last changes fastest.
Arguments:
- jacobian: bfloat16 [32, 6, 128, 3, 256], P(('pts', 'grp')), may hold values from -0.21875 to 0.21875
- point_blocks: float32 [32, 6, 256], P(('pts', 'grp')), may hold values from -0.5 to 4, as said below
- point_grad: bfloat16 [32, 3, 256], P(('pts', 'grp')), may hold values from -6 to 6
- camera_grad: float32 [32, 128], P(('pts', 'grp')), may hold values from -6 to 6
- damping: float32 [32, 128], replicated, may hold values from 1 to 8
- incidence: int32 [32, 6], P(('pts', 'grp')), may hold values from 0 to 31, as said below
- tile_owner: int32 [8], replicated, may hold values from 0 to 7, each once
- front_first: int32 [1], replicated, may hold values from 0 to 31
Outputs:
- tiles_out: float32 [256, 128, 128], P(('pts', 'grp'))
- rhs_out: float32 [32, 128], P(('pts', 'grp'))
- front_panel: float32 [2304, 512], P(None, 'grp')
Inputs may be any that keep to these rules, and one draw needn't show every extreme that they name: `incidence`: point cluster p names 6 different camera clusters, all among (p + t) mod 32 for t from 0 to 7. `point_blocks`: each point's diagonal entries exceed the sum of the magnitudes of the two off-diagonal entries of their row by 0.1 or more. `tile_owner`: A permutation of the pts indices.
All inputs are finite; a program needn't handle non-finite values.
Results may differ from a plain program's by a relative error of at most 0.0022.
Values sent between devices are 32-bit elements; how exact they have to be, the bound alone decides.
No kernel may reach another device: no remote copies, remote signals or barrier semaphores. Data moves between devices by JAX's collectives and lax.ppermute only.
A program may use at most 128 MiB of HBM per device.

v0:
```python
import jax
import jax.numpy as jnp
import numpy as np
from jax import lax
from jax.sharding import PartitionSpec as P

TOUCH = 6
BAND = 8
FRONT = 4
PRECISE = lax.Precision.HIGHEST


def shifted(value, axis, steps):
    count = lax.axis_size(axis)
    pairs = [(source, (source + steps) % count) for source in range(count)]
    return lax.ppermute(value, axis, pairs)


def invert_blocks(blocks):
    diag_x = blocks[:, 0]
    diag_y = blocks[:, 1]
    diag_z = blocks[:, 2]
    cross_xy = blocks[:, 3]
    cross_xz = blocks[:, 4]
    cross_yz = blocks[:, 5]
    adj_xx = diag_y * diag_z - cross_yz * cross_yz
    adj_yy = diag_x * diag_z - cross_xz * cross_xz
    adj_zz = diag_x * diag_y - cross_xy * cross_xy
    adj_xy = cross_xz * cross_yz - cross_xy * diag_z
    adj_xz = cross_xy * cross_yz - diag_y * cross_xz
    adj_yz = cross_xy * cross_xz - diag_x * cross_yz
    determinant = diag_x * adj_xx + cross_xy * adj_xy + cross_xz * adj_xz
    inverse_det = 1.0 / determinant
    return [
        [adj_xx * inverse_det, adj_xy * inverse_det, adj_xz * inverse_det],
        [adj_xy * inverse_det, adj_yy * inverse_det, adj_yz * inverse_det],
        [adj_xz * inverse_det, adj_yz * inverse_det, adj_zz * inverse_det],
    ]


def scale_jacobian(jacobian, blocks):
    inverse = invert_blocks(blocks)
    widened = jacobian.astype(jnp.float32)
    columns = []
    for target in range(3):
        summed = widened[:, :, :, 0, :] * inverse[0][target][:, None, None, :]
        summed = summed + widened[:, :, :, 1, :] * inverse[1][target][:, None, None, :]
        summed = summed + widened[:, :, :, 2, :] * inverse[2][target][:, None, None, :]
        columns.append(summed)
    return jnp.stack(columns, axis=3).astype(jnp.bfloat16)


def band_table(reach_rows, reach_sum):
    row_list = []
    offset_list = []
    for row_pos in range(reach_rows):
        for offset in range(BAND):
            if row_pos + offset <= reach_sum:
                row_list.append(row_pos)
                offset_list.append(offset)
    return (np.array(row_list), np.array(offset_list))


def route_rows(tiles, tile_owner, base, row_list, offset_list, pts_count):
    offsets = BAND * row_list + offset_list
    capacity = int(offsets.max()) // pts_count + 1
    residue = jnp.mod(base + jnp.asarray(offsets), pts_count)
    target = tile_owner[residue] * capacity + jnp.asarray(offsets // pts_count)
    sending = (jnp.arange(pts_count * capacity)[:, None] == target[None, :]).astype(jnp.float32)
    return (jnp.einsum("dt,trc->drc", sending, tiles, precision=PRECISE), capacity)


def collect_rows(
    incoming, capacity, perm_inverse, anchors, usable_test, clusters, grp_count, pts_count
):
    sender = jnp.arange(pts_count * capacity) // capacity
    slot_of = jnp.arange(pts_count * capacity) % capacity
    sender_anchor = anchors(sender)
    arrived = jnp.mod(perm_inverse - BAND * sender_anchor, pts_count) + slot_of * pts_count
    row_pos = arrived // BAND
    offset = arrived % BAND
    usable = usable_test(row_pos, offset)
    home_row = jnp.mod(sender_anchor + row_pos, clusters)
    owner_slot = (BAND * home_row + offset) // pts_count
    gathering = (
        (jnp.arange(BAND * grp_count)[:, None] == owner_slot[None, :]) & usable[None, :]
    ).astype(jnp.float32)
    return jnp.einsum("ms,src->mrc", gathering, incoming, precision=PRECISE)


def per_device(
    jacobian, point_blocks, point_grad, camera_grad, damping, incidence, tile_owner, front_first
):
    pts_count = lax.axis_size("pts")
    grp_count = lax.axis_size("grp")
    clusters = pts_count * grp_count
    my_grp = lax.axis_index("grp")
    my_pts = lax.axis_index("pts")
    device = my_pts * grp_count + my_grp
    local_count = jacobian.shape[0]
    cam_rows = jacobian.shape[2]
    point_cols = 3 * jacobian.shape[4]
    window_len = 2 * BAND - 2 + FRONT
    reach = 2 * BAND - 1
    scaled = scale_jacobian(jacobian, point_blocks).reshape(
        local_count, TOUCH, cam_rows, point_cols
    )
    jac_flat = jacobian.reshape(local_count, TOUCH, cam_rows, point_cols)
    local_slot = jnp.mod(incidence - device, clusters)
    placing = (local_slot[:, None, :] == jnp.arange(BAND)[None, :, None]).astype(jnp.bfloat16)
    placed_scaled = jnp.einsum(
        "ptk,pkrx->ptrx", placing, scaled, preferred_element_type=jnp.float32
    ).astype(jnp.bfloat16)
    placed_jac = jnp.einsum(
        "ptk,pkrx->ptrx", placing, jac_flat, preferred_element_type=jnp.float32
    ).astype(jnp.bfloat16)
    band_grid = jnp.einsum(
        "ptrx,pqcx->tqrc", placed_scaled, placed_jac, preferred_element_type=jnp.float32
    )
    band_rhs = jnp.einsum(
        "ptrx,px->tr",
        placed_scaled,
        point_grad.reshape(local_count, point_cols),
        preferred_element_type=jnp.float32,
    )
    perm_inverse = jnp.sum(jnp.arange(pts_count) * (tile_owner == my_pts))
    row_list, offset_list = band_table(BAND, BAND - 1)
    band_tiles = band_grid[row_list, row_list + offset_list]
    quarters = lax.all_to_all(band_tiles, "grp", split_axis=1, concat_axis=0, tiled=True)
    reach_union = BAND + grp_count - 2
    union_rows_list, union_offsets = band_table(reach_union + 1, reach_union)
    lookup = {}
    for position in range(len(union_rows_list)):
        lookup[int(union_rows_list[position]), int(union_offsets[position])] = position
    merge_table = np.zeros((len(union_rows_list), grp_count * len(row_list)), np.float32)
    for source_grp in range(grp_count):
        for position in range(len(row_list)):
            merge_table[
                lookup[source_grp + int(row_list[position]), int(offset_list[position])],
                source_grp * len(row_list) + position,
            ] = 1.0
    union_rows = jnp.einsum("us,src->urc", jnp.asarray(merge_table), quarters, precision=PRECISE)
    outgoing, capacity = route_rows(
        union_rows, tile_owner, BAND * grp_count * my_pts, union_rows_list, union_offsets, pts_count
    )
    incoming = lax.all_to_all(outgoing, "pts", split_axis=0, concat_axis=0, tiled=True)
    owner_rows = collect_rows(
        incoming,
        capacity,
        perm_inverse,
        lambda sender: sender * grp_count,
        lambda row_pos, offset: row_pos + offset <= reach_union,
        clusters,
        grp_count,
        pts_count,
    )
    owned = lax.all_to_all(owner_rows, "grp", split_axis=0, concat_axis=1, tiled=True)
    tile_id = perm_inverse + pts_count * (BAND * my_grp + jnp.arange(BAND))
    home_row = tile_id // BAND
    offset = tile_id % BAND
    other_row = jnp.mod(home_row + offset, clusters)
    pick_damp = (home_row[:, None] == jnp.arange(clusters)[None, :]).astype(jnp.float32)
    damp_rows = jnp.dot(pick_damp, damping, precision=PRECISE)
    identity = jnp.eye(cam_rows, dtype=jnp.float32)
    owned = owned + jnp.where(
        (offset == 0)[:, None, None], damp_rows[:, :, None] * identity[None, :, :], 0.0
    )
    summed = band_rhs[0]
    for step in range(1, BAND):
        summed = summed + shifted(band_rhs[step], ("pts", "grp"), step)
    reduced = camera_grad - summed[None, :]
    front_start = front_first[0]
    window_base = front_start - (BAND - 1)
    pos_home = jnp.mod(home_row - window_base, clusters)
    pos_other = jnp.mod(other_row - window_base, clusters)
    front_axis = jnp.arange(FRONT)[:, None, None]
    reach_axis = jnp.arange(reach)[None, :, None]
    direct = (
        (pos_other[None, None, :] == BAND - 1 + front_axis)
        & (pos_home[None, None, :] == front_axis + reach_axis)
    ).astype(jnp.float32)
    mirror = (
        (pos_home[None, None, :] == BAND - 1 + front_axis)
        & (offset[None, None, :] > 0)
        & (pos_other[None, None, :] == front_axis + reach_axis)
    ).astype(jnp.float32)
    front_rows = jnp.einsum("kes,sab->keab", direct, owned, precision=PRECISE) + jnp.einsum(
        "kes,sba->keab", mirror, owned, precision=PRECISE
    )
    my_pos = jnp.mod(device - window_base, clusters)
    window_rhs = (jnp.arange(window_len)[:, None] == my_pos).astype(jnp.float32) * reduced
    front_rows, window_rhs = lax.psum((front_rows, window_rhs), ("pts", "grp"))
    flat_rows = jnp.concatenate(
        [
            front_rows.reshape(FRONT * reach, cam_rows, cam_rows),
            jnp.zeros((1, cam_rows, cam_rows), jnp.float32),
        ],
        axis=0,
    )
    lookup_table = np.full((window_len, FRONT), FRONT * reach, np.int32)
    for position in range(window_len):
        for front_pos in range(FRONT):
            if 0 <= position - front_pos < reach:
                lookup_table[position, front_pos] = front_pos * reach + position - front_pos
    columns = (
        flat_rows[lookup_table]
        .transpose(0, 2, 1, 3)
        .reshape(window_len * cam_rows, FRONT * cam_rows)
    )
    square = columns[(BAND - 1) * cam_rows : (BAND - 1 + FRONT) * cam_rows]
    factor = jnp.linalg.cholesky(square)
    panel = jax.scipy.linalg.solve_triangular(factor, columns.T, lower=True).T
    share = FRONT * cam_rows // grp_count
    front_panel = lax.dynamic_slice_in_dim(panel, my_grp * share, share, 1)
    panel_blocks = panel.reshape(window_len, cam_rows, FRONT * cam_rows)

    def inside_rest(position):
        return (position < window_len) & ((position < BAND - 1) | (position >= BAND - 1 + FRONT))

    update_mask = inside_rest(pos_home) & inside_rest(pos_other)
    pick_home = (pos_home[:, None] == jnp.arange(window_len)[None, :]).astype(jnp.float32)
    pick_other = (pos_other[:, None] == jnp.arange(window_len)[None, :]).astype(jnp.float32)
    rows_home = jnp.einsum("sp,pra->sra", pick_home, panel_blocks, precision=PRECISE)
    rows_other = jnp.einsum("sp,pra->sra", pick_other, panel_blocks, precision=PRECISE)
    change = jnp.einsum("sra,sca->src", rows_home, rows_other, precision=PRECISE)
    tiles_out = owned - jnp.where(update_mask[:, None, None], change, 0.0)
    solved_front = jax.scipy.linalg.solve_triangular(
        factor, window_rhs[BAND - 1 : BAND - 1 + FRONT].reshape(FRONT * cam_rows), lower=True
    )
    my_row = lax.dynamic_index_in_dim(
        panel_blocks, jnp.clip(my_pos, 0, window_len - 1), 0, keepdims=False
    )
    correction = reduced[0] - jnp.dot(my_row, solved_front, precision=PRECISE)
    front_piece = lax.dynamic_index_in_dim(
        solved_front.reshape(FRONT, cam_rows),
        jnp.clip(my_pos - (BAND - 1), 0, FRONT - 1),
        0,
        keepdims=False,
    )
    in_front = (my_pos >= BAND - 1) & (my_pos < BAND - 1 + FRONT)
    in_window = my_pos < window_len
    rhs_out = jnp.where(in_front, front_piece, jnp.where(in_window, correction, reduced[0]))[
        None, :
    ]
    return (tiles_out, rhs_out, front_panel)


def solution(mesh):
    in_specs = (
        P(("pts", "grp"), None, None, None, None),
        P(("pts", "grp"), None, None),
        P(("pts", "grp"), None, None),
        P(("pts", "grp"), None),
        P(),
        P(("pts", "grp"), None),
        P(),
        P(),
    )
    out_specs = (P(("pts", "grp"), None, None), P(("pts", "grp"), None), P(None, "grp"))
    return jax.shard_map(
        per_device, mesh=mesh, in_specs=in_specs, out_specs=out_specs, check_vma=False
    )
```

profile of v0, /device:TPU:0, one launch (start us, length us, event | category | flops | bytes accessed | tf_op | source)
XLA Modules:
  0.0 489.5 jit_solution(7508762552952673536)
XLA Ops:
  27.1 4.4 all-to-all-start
  32.1 5.0 %fusion.120 = s32[60]{0:T(128)S(1)} fusion(s32[60]{0:T(128)S(1)} %copy-done.16, s32[60]{0:T(128)S(1)} %copy-done.15, s32[]{:T(128)} %bitcast.1, s32[]{:T(128)} %bitcast.2, s32[]{:T(128)} %bitcast.3, s32[]{:T(128)} %bitcast.4, s32[]{:T(128)} %bitcast.5, s32[]{:T(128)} %bitcast.6, s32[]{:T(128)} %bitcast.7, s32[]{:T(128)} %bitcast.8, s32[]{:T(128)S(6)} %mul.589), kind=kLoop, calls=%fused_computation.234 | loop fusion | flops 1860 | bytes 756 | tf_op jit(solution)/shard_map/add | solution.py:68
  37.1 25.7 %all-to-all-done = f32[36,128,128]{2,0,1:T(8,128)S(1)} async-done(((f32[36,128,128]{2,0,1:T(8,128)}), f32[36,128,128]{2,0,1:T(8,128)S(1)}, u32[]{:S(2)}, u32[]{:S(2)}) %all-to-all-start) | async-done | bytes 2359328 | tf_op jit(solution)/shard_map/all_to_all | solution.py:129
  68.2 6.6 %all-to-all-start.1 = ((f32[88,32,128]{2,1,0:T(8,128)}), f32[88,32,128]{2,1,0:T(8,128)S(1)}, u32[]{:S(2)}, u32[]{:S(2)}) async-start(f32[88,32,128]{2,1,0:T(8,128)} %copy.52), calls=%async_computation.1 | async-start | bytes 2883584 | tf_op jit(solution)/shard_map/all_to_all | solution.py:146
  78.3 30.5 %all-to-all-done.1 = f32[88,32,128]{2,1,0:T(8,128)S(1)} async-done(((f32[88,32,128]{2,1,0:T(8,128)}), f32[88,32,128]{2,1,0:T(8,128)S(1)}, u32[]{:S(2)}, u32[]{:S(2)}) %all-to-all-start.1) | async-done | bytes 1441824 | tf_op jit(solution)/shard_map/all_to_all | solution.py:146
  114.8 10.1 %all-reduce.4.cloned.1.call-start = ((), (), s32[]{:S(2)}) async-start(), calls=%async_computation.3 | async-start | bytes 7864320 | tf_op jit(solution)/shard_map/psum | solution.py:192
  151.3 38.8 %psum.15 = f32[18,128]{1,0:T(8,128)S(1)} all-reduce(f32[18,128]{1,0:T(8,128)S(1)} %broadcast_multiply_fusion), channel_id=1, replica_groups=mesh['pts'=8,'grp'=4] {'pts','grp'}, use_global_device_ids=true, to_apply=%region_10.11 | all-reduce | flops 2304 | bytes 18432 | tf_op jit(solution)/shard_map/psum | solution.py:192
  190.1 83.9 %all-reduce.4.cloned.1.call-done = f32[60,128,128]{2,1,0:T(8,128)} async-done(((f32[60,128,128]{2,1,0:T(8,128)}), f32[60,128,128]{2,1,0:T(8,128)}) %all-reduce.4.cloned.1.call-update) | async-done | bytes 3932176 | tf_op jit(solution)/shard_map/psum | solution.py:192
  274.0 4.5 concatenate.34
  278.5 5.2 %gather_fusion.1 = f32[72,128,128]{2,1,0:T(8,128)} fusion(f32[61,128,128]{2,1,0:T(8,128)} %concatenate.34, s32[1024]{0:T(1024)S(1)} %pad_clamp_fusion), kind=kCustom, calls=%fused_computation.1 | custom fusion | bytes 9437472 | tf_op jit(solution)/shard_map/gather | solution.py:206
  289.2 11.7 %cholesky.86 = f32[128,128]{1,0:T(8,128)S(1)} custom-call(f32[128,128]{1,0:T(8,128)S(1)} %cholesky.232), custom_call_target="Cholesky" | custom-call | tf_op jit(solution)/shard_map/jit(cholesky)/cholesky | solution.py:211
  301.1 6.5 %copy.75 = f32[18,128,4,128]{1,0,3,2:T(8,128)} copy(f32[18,128,4,128]{3,1,2,0:T(8,128)} %bitcast.269) | data formatting | bytes 9437184 | tf_op jit(solution)/shard_map/reshape | solution.py:208
  307.6 9.8 %custom-call.34 = f32[1,128,128]{1,2,0:T(8,128)S(1)} custom-call(f32[1,128,128]{2,1,0:T(8,128)S(1)} %get-tuple-element.50), custom_call_target="InvertDiagBlocksLowerTriangular" | custom-call | tf_op jit(solution)/shard_map/jit(cholesky)/cholesky | solution.py:211
  318.1 11.7 %cholesky.183 = f32[128,128]{1,0:T(8,128)S(1)} custom-call(f32[128,128]{1,0:T(8,128)S(1)} %cholesky.236), custom_call_target="Cholesky" | custom-call | tf_op jit(solution)/shard_map/jit(cholesky)/cholesky | solution.py:211
  331.2 9.8 %custom-call.35 = f32[1,128,128]{1,2,0:T(8,128)S(1)} custom-call(f32[1,128,128]{2,1,0:T(8,128)S(1)} %get-tuple-element.47), custom_call_target="InvertDiagBlocksLowerTriangular" | custom-call | tf_op jit(solution)/shard_map/jit(cholesky)/cholesky | solution.py:211
  341.6 12.1 %cholesky.204 = f32[128,128]{1,0:T(8,128)S(1)} custom-call(f32[128,128]{1,0:T(8,128)S(1)} %cholesky.241), custom_call_target="Cholesky" | custom-call | tf_op jit(solution)/shard_map/jit(cholesky)/cholesky | solution.py:211
  354.4 9.8 %custom-call.36 = f32[1,128,128]{1,2,0:T(8,128)S(1)} custom-call(f32[1,128,128]{2,1,0:T(8,128)S(1)} %get-tuple-element.44), custom_call_target="InvertDiagBlocksLowerTriangular" | custom-call | tf_op jit(solution)/shard_map/jit(cholesky)/cholesky | solution.py:211
  364.8 11.7 %cholesky.221 = f32[128,128]{1,0:T(8,128)S(1)} custom-call(f32[128,128]{1,0:T(8,128)S(1)} %convolution_subtract_fusion.5), custom_call_target="Cholesky" | custom-call | tf_op jit(solution)/shard_map/jit(cholesky)/cholesky | solution.py:211
  379.9 8.0 %while.1 = (s32[]{:T(128)}, f32[512,512]{1,0:T(8,128)S(1)}, s32[4,2]{0,1:T(2,128)S(1)}, f32[4,128,128]{2,1,0:T(8,128)S(1)}, s32[]{:T(128)}) while((s32[]{:T(128)}, f32[512,512]{1,0:T(8,128)S(1)}, s32[4,2]{0,1:T(2,128)S(1)}, f32[4,128,128]{2,1,0:T(8,128)S(1)}, s32[]{:T(128)}) %tuple.64), condition=%wide.while_cond, body=%wide.while_body.sunk | while | flops 2 | bytes 131181 | solution.py:212
  387.9 39.5 %custom-call.37 = f32[4,128,128]{1,2,0:T(8,128)S(1)} custom-call(f32[4,128,128]{2,1,0:T(8,128)S(1)} %get-tuple-element.10), custom_call_target="InvertDiagBlocksLowerTriangular" | custom-call | tf_op jit(solution)/shard_map/jit(_solve_triangular)/triangular_solve | solution.py:212
  444.9 6.1 %copy.63 = f32[2304,512]{1,0:T(8,128)} copy(f32[2304,512]{0,1:T(8,128)} %get-tuple-element.37) | data formatting | bytes 9437184 | tf_op jit(solution)/shard_map/transpose | solution.py:212
  451.0 7.7 %fusion.2 = f32[8,128,512]{2,0,1:T(8,128)S(1)} fusion(f32[18,128,512]{2,1,0:T(8,128)} %bitcast.264, s32[8]{0:T(128)S(1)} %get-tuple-element.30), kind=kOutput, calls=%fused_computation.6 | convolution fusion | flops 113246352 | bytes 6815776 | tf_op jit(solution)/shard_map/sp,pra->sra/dot_general | solution.py:223
  458.6 5.9 %fusion = f32[8,128,512]{2,0,1:T(8,128)} fusion(f32[18,128,512]{2,1,0:T(8,128)S(1)} %bitcast.266, s32[8]{0:T(128)S(1)} %get-tuple-element.29), kind=kOutput, calls=%fused_computation.4 | convolution fusion | flops 113246352 | bytes 6815776 | tf_op jit(solution)/shard_map/sp,pra->sra/dot_general | solution.py:224
  473.8 6.7 %fusion.28 = f32[8,128,128]{2,1,0:T(8,128)} fusion(f32[8,128,128]{2,1,0:T(8,128)S(1)} %bitcast_add_fusion.2, f32[8,128,512]{2,0,1:T(8,128)} %fusion, f32[8,128,512]{2,0,1:T(8,128)S(1)} %fusion.2, pred[8]{0:T(512)(128)(4,1)S(1)} %get-tuple-element.28), kind=kOutput, calls=%fused_computation.37 | convolution fusion | flops 805568512 | bytes 5242888 | tf_op jit(solution)/shard_map/sra,sca->src/dot_general | solution.py:225
  (158 shorter events, 107.7 us)
Async XLA Ops:
  7.2 118.4 %copy-start = (f32[32,128]{1,0:T(8,128)S(1)}, f32[32,128]{1,0:T(8,128)}, u32[]{:S(2)}) copy-start(f32[32,128]{1,0:T(8,128)} %param.21) | copy-start | bytes 49156
  13.8 2.0 copy-start.17
  18.5 3.5 copy-start.9
  27.1 4.4 copy-start.11
  27.1 5.0 %copy-start.15 = (s32[60]{0:T(128)S(1)}, s32[60]{0:T(128)}, u32[]{:S(2)}) copy-start(s32[60]{0:T(128)} %constant.368.clone) | copy-start | bytes 724
  27.1 5.0 %copy-start.16 = (s32[60]{0:T(128)S(1)}, s32[60]{0:T(128)}, u32[]{:S(2)}) copy-start(s32[60]{0:T(128)} %constant.369.clone) | copy-start | bytes 724
  27.1 35.7 %all-to-all-start = ((f32[36,128,128]{2,0,1:T(8,128)}), f32[36,128,128]{2,0,1:T(8,128)S(1)}, u32[]{:S(2)}, u32[]{:S(2)}) async-start(f32[36,128,128]{2,0,1:T(8,128)} %copy.49), calls=%async_computation | async-start | bytes 5242880 | tf_op jit(solution)/shard_map/all_to_all | solution.py:129
  37.1 26.2 %copy-start.10 = (f32[60,144,1]{1,0,2:T(8,128)S(1)}, f32[60,144,1]{1,0,2:T(8,128)}, u32[]{:S(2)}) copy-start(f32[60,144,1]{1,0,2:T(8,128)} %constant.431) | copy-start | bytes 103684
  68.2 40.5 %all-to-all-start.1 = ((f32[88,32,128]{2,1,0:T(8,128)}), f32[88,32,128]{2,1,0:T(8,128)S(1)}, u32[]{:S(2)}, u32[]{:S(2)}) async-start(f32[88,32,128]{2,1,0:T(8,128)} %copy.52), calls=%async_computation.1 | async-start | bytes 2883584 | tf_op jit(solution)/shard_map/all_to_all | solution.py:146
  111.3 14.4 %all-to-all-start.2 = ((f32[32,32,128]{2,1,0:T(8,128)}), f32[32,32,128]{2,1,0:T(8,128)S(1)}, u32[]{:S(2)}, u32[]{:S(2)}) async-start(f32[32,32,128]{2,1,0:T(8,128)} %copy.54), calls=%async_computation.2 | async-start | bytes 1048576 | tf_op jit(solution)/shard_map/all_to_all | solution.py:157
  114.8 159.2 %all-reduce.4.cloned.1.call-start = ((), (), s32[]{:S(2)}) async-start(), calls=%async_computation.3 | async-start | bytes 7864320 | tf_op jit(solution)/shard_map/psum | solution.py:192
  133.9 8.4 %copy-start.14 = (s32[72]{0:T(128)S(1)}, s32[72]{0:T(128)}, u32[]{:S(2)}) copy-start(s32[72]{0:T(128)} %constant.430) | copy-start | bytes 868
  133.9 17.3 %copy-start.13 = (f32[1,128]{1,0:T(1,128)S(1)}, f32[1,128]{1,0:T(1,128)}, u32[]{:S(2)}) copy-start(f32[1,128]{1,0:T(1,128)} %param.20) | copy-start | bytes 1540
  138.3 6.6 %collective-permute-start = (f32[128]{0:T(128)S(1)}, f32[128]{0:T(128)S(1)}, u32[]{:S(2)}, u32[]{:S(2)}) collective-permute-start(f32[128]{0:T(128)S(1)} %get-tuple-element.57), channel_id=1, source_target_pairs={{0,1},{1,2},{2,3},{3,4},{4,5},{5,6},{6,7},{7,8},{8,9},{9,10},{10,1... | collective-permute-start | bytes 1544 | tf_op jit(solution)/shard_map/ppermute | solution.py:16
  138.5 7.3 %collective-permute-start.1 = (f32[128]{0:T(128)S(1)}, f32[128]{0:T(128)S(1)}, u32[]{:S(2)}, u32[]{:S(2)}) collective-permute-start(f32[128]{0:T(128)S(1)} %get-tuple-element.63), channel_id=1, source_target_pairs={{0,2},{1,3},{2,4},{3,5},{4,6},{5,7},{6,8},{7,9},{8,10},{9,11},{10,... | collective-permute-start | bytes 1544 | tf_op jit(solution)/shard_map/ppermute | solution.py:16
  140.1 7.4 %collective-permute-start.2 = (f32[128]{0:T(128)S(1)}, f32[128]{0:T(128)S(1)}, u32[]{:S(2)}, u32[]{:S(2)}) collective-permute-start(f32[128]{0:T(128)S(1)} %get-tuple-element.62), channel_id=1, source_target_pairs={{0,3},{1,4},{2,5},{3,6},{4,7},{5,8},{6,9},{7,10},{8,11},{9,12},{10... | collective-permute-start | bytes 1544 | tf_op jit(solution)/shard_map/ppermute | solution.py:16
  142.3 6.3 %collective-permute-start.3 = (f32[128]{0:T(128)S(1)}, f32[128]{0:T(128)S(1)}, u32[]{:S(2)}, u32[]{:S(2)}) collective-permute-start(f32[128]{0:T(128)S(1)} %get-tuple-element.61), channel_id=1, source_target_pairs={{0,4},{1,5},{2,6},{3,7},{4,8},{5,9},{6,10},{7,11},{8,12},{9,13},{1... | collective-permute-start | bytes 1544 | tf_op jit(solution)/shard_map/ppermute | solution.py:16
  142.3 6.3 %collective-permute-start.4 = (f32[128]{0:T(128)S(1)}, f32[128]{0:T(128)S(1)}, u32[]{:S(2)}, u32[]{:S(2)}) collective-permute-start(f32[128]{0:T(128)S(1)} %get-tuple-element.60), channel_id=1, source_target_pairs={{0,5},{1,6},{2,7},{3,8},{4,9},{5,10},{6,11},{7,12},{8,13},{9,14},{... | collective-permute-start | bytes 1544 | tf_op jit(solution)/shard_map/ppermute | solution.py:16
  144.9 6.3 %collective-permute-start.5 = (f32[128]{0:T(128)S(1)}, f32[128]{0:T(128)S(1)}, u32[]{:S(2)}, u32[]{:S(2)}) collective-permute-start(f32[128]{0:T(128)S(1)} %get-tuple-element.59), channel_id=1, source_target_pairs={{0,6},{1,7},{2,8},{3,9},{4,10},{5,11},{6,12},{7,13},{8,14},{9,15},... | collective-permute-start | bytes 1544 | tf_op jit(solution)/shard_map/ppermute | solution.py:16
  145.8 5.4 %collective-permute-start.6 = (f32[128]{0:T(128)S(1)}, f32[128]{0:T(128)S(1)}, u32[]{:S(2)}, u32[]{:S(2)}) collective-permute-start(f32[128]{0:T(128)S(1)} %get-tuple-element.58), channel_id=1, source_target_pairs={{0,7},{1,8},{2,9},{3,10},{4,11},{5,12},{6,13},{7,14},{8,15},{9,16}... | collective-permute-start | bytes 1544 | tf_op jit(solution)/shard_map/ppermute | solution.py:16
  301.1 16.4 %copy-start.8 = (f32[512,512]{1,0:T(8,128)S(1)}, f32[512,512]{1,0:T(8,128)}, u32[]{:S(2)}) copy-start(f32[512,512]{1,0:T(8,128)} %copy-done.7) | copy-start | bytes 3145732
  387.9 49.3 %copy-start.6 = (f32[512,512]{1,0:T(8,128)}, f32[512,512]{1,0:T(8,128)S(1)}, u32[]{:S(2)}) copy-start(f32[512,512]{1,0:T(8,128)S(1)} %get-tuple-element.133) | copy-start | bytes 3145732
  451.0 7.7 %copy-start.2 = (f32[2304,512]{1,0:T(8,128)S(1)}, f32[2304,512]{1,0:T(8,128)}, u32[]{:S(2)}) copy-start(f32[2304,512]{1,0:T(8,128)} %copy.63) | copy-start | bytes 14155780
  473.8 8.5 %copy-start.1 = (f32[32,128]{1,0:T(8,128)S(1)}, f32[32,128]{1,0:T(8,128)}, u32[]{:S(2)}) copy-start(f32[32,128]{1,0:T(8,128)} %param.21) | copy-start | bytes 49156
  (5 other events, 5.7 us)
Sparse Core Ops, SparseCore 0:
  133.4 140.5 all-reduce.3
where the time goes:
time: 499 us; the launch traced here: 490 us
  waiting for transfers between devices  147 us (29%)
  other arithmetic  134 us (27%)
  local copies, waits for them, and re-layouts  66.2 us (13%)
  matrix products  54.6 us (11%)
  blocking collectives  38.8 us (8%)
  starting transfers between devices  30.4 us (6%)
  between operations  18.1 us (4%)
    psum x1, waiting for transfers between devices, per_device(): front_rows, window_rhs = lax.psum((front_rows, window_rhs), ('pts', 'grp'))  83.9 us
    another operation x15, other arithmetic, per_device(): factor = jnp.linalg.cholesky(square)  79.4 us
    another operation x4, other arithmetic, per_device(): panel = jax.scipy.linalg.solve_triangular(factor, columns.T, lower=True).T  43.9 us
    psum x1, blocking collectives, per_device(): front_rows, window_rhs = lax.psum((front_rows, window_rhs), ('pts', 'grp'))  38.8 us
    all_to_all x1, waiting for transfers between devices, per_device(): lax.all_to_all(outgoing, 'pts', split_axis=0, concat_axis=0, tiled=True)  30.5 us
    all_to_all x1, waiting for transfers between devices, per_device(): lax.all_to_all(band_tiles, 'grp', split_axis=1, concat_axis=0, tiled=True)  25.7 us
    unnamed x40, local copies, waits for them, and re-layouts  13.1 us
    psum x1, starting transfers between devices, per_device(): front_rows, window_rhs = lax.psum((front_rows, window_rhs), ('pts', 'grp'))  10.1 us
  transfers between devices with their start and end apart: 11, of which 7 were waited for; matrix products, arithmetic and copies ran while one was open for 3% of the time, Pallas kernels for 0%

commit v1 on v0

--- a/solution.py
+++ b/solution.py
@@ -126,7 +126,15 @@
     perm_inverse = jnp.sum(jnp.arange(pts_count) * (tile_owner == my_pts))
     row_list, offset_list = band_table(BAND, BAND - 1)
     band_tiles = band_grid[row_list, row_list + offset_list]
-    quarters = lax.all_to_all(band_tiles, "grp", split_axis=1, concat_axis=0, tiled=True)
+    quarters = jnp.concatenate(
+        jax.lax.all_to_all(
+            jnp.stack(jnp.split(band_tiles, jax.lax.axis_size("grp"), 1), 0),
+            axis_name="grp",
+            split_axis=0,
+            concat_axis=0,
+        ),
+        0,
+    )
     reach_union = BAND + grp_count - 2
     union_rows_list, union_offsets = band_table(reach_union + 1, reach_union)
     lookup = {}

time: 499 us -> 518 us (1.038)
  local copies, waits for them, and re-layouts: 66.2 us -> 77.1 us
    another operation x14 -> x19, local copies, waits for them, and re-layouts: 9.91 us -> 23.4 us  [the longest x5 13.5 us: per_device(): jnp.stack(jnp.split(band_tiles, jax.lax.axis_size('grp'), 1), 0)]
    all_to_all x1, starting transfers between devices: 6.65 us -> 17.8 us  [per_device(): lax.all_to_all(outgoing, 'pts', split_axis=0, concat_axis=0, tiled=True)]
    psum x1, starting transfers between devices: 10.1 us -> 0.04 us  [per_device(): front_rows, window_rhs = lax.psum((front_rows, window_rhs), ('pts', 'grp'))]
    all_to_all x1, waiting for transfers between devices: 0.01 us -> 7.85 us  [per_device(): lax.all_to_all(owner_rows, 'grp', split_axis=0, concat_axis=1, tiled=True)]
    unnamed x40 -> x44, local copies, waits for them, and re-layouts: 13.1 us -> 13 us
where the time goes in v1:
time: 518 us; the launch traced here: 508 us
  waiting for transfers between devices  152 us (29%)
  other arithmetic  137 us (26%)
  local copies, waits for them, and re-layouts  77.1 us (15%)
  matrix products  54.6 us (11%)
  blocking collectives  38.9 us (8%)
  starting transfers between devices  30.4 us (6%)
  between operations  18.2 us (4%)
    psum x1, waiting for transfers between devices, per_device(): front_rows, window_rhs = lax.psum((front_rows, window_rhs), ('pts', 'grp'))  82.6 us
    another operation x15, other arithmetic, per_device(): factor = jnp.linalg.cholesky(square)  79.1 us
    another operation x4, other arithmetic, per_device(): panel = jax.scipy.linalg.solve_triangular(factor, columns.T, lower=True).T  43.9 us
    psum x1, blocking collectives, per_device(): front_rows, window_rhs = lax.psum((front_rows, window_rhs), ('pts', 'grp'))  38.9 us
    all_to_all x1, waiting for transfers between devices, per_device(): lax.all_to_all(outgoing, 'pts', split_axis=0, concat_axis=0, tiled=True)  30.4 us
    all_to_all x1, waiting for transfers between devices, per_device(): jax.lax.all_to_all(jnp.stack(jnp.split(band_tiles, jax.lax.axis_size('grp...  22.6 us
    all_to_all x1, starting transfers between devices, per_device(): lax.all_to_all(outgoing, 'pts', split_axis=0, concat_axis=0, tiled=True)  17.8 us
    another operation x5, local copies, waits for them, and re-layouts, per_device(): jnp.stack(jnp.split(band_tiles, jax.lax.axis_size('grp'), 1), 0)  13.5 us
  transfers between devices with their start and end apart: 11, of which 7 were waited for; matrix products, arithmetic and copies ran while one was open for 3% of the time, Pallas kernels for 0%

profile of v1, /device:TPU:0, one launch (start us, length us, event | category | flops | bytes accessed | tf_op | source)
XLA Modules:
  0.0 508.2 jit_solution(16612316920199481232)
XLA Ops:
  24.8 5.6 %slice_bitcast_fusion.3 = (f32[1,36,32,128]{2,3,1,0:T(8,128)}, f32[1,36,32,128]{2,3,1,0:T(8,128)}, f32[1,36,32,128]{2,3,1,0:T(8,128)}, f32[1,36,32,128]{2,3,1,0:T(8,128)}) fusion(f32[36,128,128]{1,2,0:T(8,128)S(1)} %gather_fusion), kind=kLoop, calls=%fused_computation.22 | loop fusion | bytes 4718592 | tf_op jit(solution)/shard_map/stack | solution.py:131
  46.3 5.2 %fusion.120 = s32[60]{0:T(128)S(1)} fusion(s32[60]{0:T(128)S(1)} %copy-done.18, s32[60]{0:T(128)S(1)} %copy-done.17, s32[]{:T(128)} %bitcast.1, s32[]{:T(128)} %bitcast.2, s32[]{:T(128)} %bitcast.3, s32[]{:T(128)} %bitcast.4, s32[]{:T(128)} %bitcast.5, s32[]{:T(128)} %bitcast.6, s32[]{:T(128)} %bitcast.7, s32[]{:T(128)} %bitcast.8, s32[]{:T(128)S(6)} %mul.589), kind=kLoop, calls=%fused_computation.239 | loop fusion | flops 1860 | bytes 756 | tf_op jit(solution)/shard_map/add | solution.py:68
  51.5 22.6 %all-to-all-done = f32[4,36,32,128]{3,2,1,0:T(8,128)S(1)} async-done(((f32[4,36,32,128]{3,2,1,0:T(8,128)}), f32[4,36,32,128]{3,2,1,0:T(8,128)S(1)}, u32[]{:S(2)}, u32[]{:S(2)}) %all-to-all-start) | async-done | bytes 2359328 | tf_op jit(solution)/shard_map/all_to_all | solution.py:130
  79.1 17.8 %all-to-all-start.1 = ((f32[88,32,128]{2,1,0:T(8,128)}), f32[88,32,128]{2,1,0:T(8,128)S(1)}, u32[]{:S(2)}, u32[]{:S(2)}) async-start(f32[88,32,128]{2,1,0:T(8,128)} %copy.81), calls=%async_computation.1 | async-start | bytes 2883584 | tf_op jit(solution)/shard_map/all_to_all | solution.py:154
  100.2 30.4 %all-to-all-done.1 = f32[88,32,128]{2,1,0:T(8,128)S(1)} async-done(((f32[88,32,128]{2,1,0:T(8,128)}), f32[88,32,128]{2,1,0:T(8,128)S(1)}, u32[]{:S(2)}, u32[]{:S(2)}) %all-to-all-start.1) | async-done | bytes 1441824 | tf_op jit(solution)/shard_map/all_to_all | solution.py:154
  137.6 7.9 %all-to-all-done.2 = f32[32,32,128]{2,1,0:T(8,128)S(1)} async-done(((f32[32,32,128]{2,1,0:T(8,128)}), f32[32,32,128]{2,1,0:T(8,128)S(1)}, u32[]{:S(2)}, u32[]{:S(2)}) %all-to-all-start.2) | async-done | bytes 524320 | tf_op jit(solution)/shard_map/all_to_all | solution.py:165
  171.1 38.9 %psum.15 = f32[18,128]{1,0:T(8,128)S(1)} all-reduce(f32[18,128]{1,0:T(8,128)S(1)} %broadcast_multiply_fusion), channel_id=1, replica_groups=mesh['pts'=8,'grp'=4] {'pts','grp'}, use_global_device_ids=true, to_apply=%region_10.11 | all-reduce | flops 2304 | bytes 18432 | tf_op jit(solution)/shard_map/psum | solution.py:200
  210.0 82.6 %all-reduce.4.cloned.1.call-done = f32[60,128,128]{2,1,0:T(8,128)} async-done(((f32[60,128,128]{2,1,0:T(8,128)}), f32[60,128,128]{2,1,0:T(8,128)}) %all-reduce.4.cloned.1.call-update) | async-done | bytes 3932176 | tf_op jit(solution)/shard_map/psum | solution.py:200
  292.6 4.5 concatenate.34
  297.1 5.2 %gather_fusion.1 = f32[72,128,128]{2,1,0:T(8,128)} fusion(f32[61,128,128]{2,1,0:T(8,128)} %concatenate.34, s32[1024]{0:T(1024)S(1)} %pad_clamp_fusion), kind=kCustom, calls=%fused_computation.1 | custom fusion | bytes 9437472 | tf_op jit(solution)/shard_map/gather | solution.py:214
  307.8 11.7 %cholesky.86 = f32[128,128]{1,0:T(8,128)S(1)} custom-call(f32[128,128]{1,0:T(8,128)S(1)} %cholesky.232), custom_call_target="Cholesky" | custom-call | tf_op jit(solution)/shard_map/jit(cholesky)/cholesky | solution.py:219
  319.7 6.7 %copy.104 = f32[18,128,4,128]{1,0,3,2:T(8,128)} copy(f32[18,128,4,128]{3,1,2,0:T(8,128)} %bitcast.277) | data formatting | bytes 9437184 | tf_op jit(solution)/shard_map/reshape | solution.py:216
  326.5 9.8 %custom-call.34 = f32[1,128,128]{1,2,0:T(8,128)S(1)} custom-call(f32[1,128,128]{2,1,0:T(8,128)S(1)} %get-tuple-element.57), custom_call_target="InvertDiagBlocksLowerTriangular" | custom-call | tf_op jit(solution)/shard_map/jit(cholesky)/cholesky | solution.py:219
  337.0 11.7 %cholesky.183 = f32[128,128]{1,0:T(8,128)S(1)} custom-call(f32[128,128]{1,0:T(8,128)S(1)} %cholesky.236), custom_call_target="Cholesky" | custom-call | tf_op jit(solution)/shard_map/jit(cholesky)/cholesky | solution.py:219
  350.0 9.8 %custom-call.35 = f32[1,128,128]{1,2,0:T(8,128)S(1)} custom-call(f32[1,128,128]{2,1,0:T(8,128)S(1)} %get-tuple-element.54), custom_call_target="InvertDiagBlocksLowerTriangular" | custom-call | tf_op jit(solution)/shard_map/jit(cholesky)/cholesky | solution.py:219
  360.5 11.9 %cholesky.204 = f32[128,128]{1,0:T(8,128)S(1)} custom-call(f32[128,128]{1,0:T(8,128)S(1)} %cholesky.241), custom_call_target="Cholesky" | custom-call | tf_op jit(solution)/shard_map/jit(cholesky)/cholesky | solution.py:219
  373.0 9.8 %custom-call.36 = f32[1,128,128]{1,2,0:T(8,128)S(1)} custom-call(f32[1,128,128]{2,1,0:T(8,128)S(1)} %get-tuple-element.51), custom_call_target="InvertDiagBlocksLowerTriangular" | custom-call | tf_op jit(solution)/shard_map/jit(cholesky)/cholesky | solution.py:219
  383.5 11.7 %cholesky.221 = f32[128,128]{1,0:T(8,128)S(1)} custom-call(f32[128,128]{1,0:T(8,128)S(1)} %convolution_subtract_fusion.5), custom_call_target="Cholesky" | custom-call | tf_op jit(solution)/shard_map/jit(cholesky)/cholesky | solution.py:219
  398.5 8.0 %while.1 = (s32[]{:T(128)}, f32[512,512]{1,0:T(8,128)S(1)}, s32[4,2]{0,1:T(2,128)S(1)}, f32[4,128,128]{2,1,0:T(8,128)S(1)}, s32[]{:T(128)}) while((s32[]{:T(128)}, f32[512,512]{1,0:T(8,128)S(1)}, s32[4,2]{0,1:T(2,128)S(1)}, f32[4,128,128]{2,1,0:T(8,128)S(1)}, s32[]{:T(128)}) %tuple.68), condition=%wide.while_cond, body=%wide.while_body.sunk | while | flops 2 | bytes 131181 | solution.py:220
  406.5 39.5 %custom-call.37 = f32[4,128,128]{1,2,0:T(8,128)S(1)} custom-call(f32[4,128,128]{2,1,0:T(8,128)S(1)} %get-tuple-element.10), custom_call_target="InvertDiagBlocksLowerTriangular" | custom-call | tf_op jit(solution)/shard_map/jit(_solve_triangular)/triangular_solve | solution.py:220
  463.5 6.1 %copy.92 = f32[2304,512]{1,0:T(8,128)} copy(f32[2304,512]{0,1:T(8,128)} %get-tuple-element.40) | data formatting | bytes 9437184 | tf_op jit(solution)/shard_map/transpose | solution.py:220
  469.6 7.7 %fusion.2 = f32[8,128,512]{2,0,1:T(8,128)S(1)} fusion(f32[18,128,512]{2,1,0:T(8,128)} %bitcast.272, s32[8]{0:T(128)S(1)} %get-tuple-element.33), kind=kOutput, calls=%fused_computation.6 | convolution fusion | flops 113246352 | bytes 6815776 | tf_op jit(solution)/shard_map/sp,pra->sra/dot_general | solution.py:231
  477.3 5.9 %fusion = f32[8,128,512]{2,0,1:T(8,128)} fusion(f32[18,128,512]{2,1,0:T(8,128)S(1)} %bitcast.274, s32[8]{0:T(128)S(1)} %get-tuple-element.32), kind=kOutput, calls=%fused_computation.4 | convolution fusion | flops 113246352 | bytes 6815776 | tf_op jit(solution)/shard_map/sp,pra->sra/dot_general | solution.py:232
  492.4 6.7 %fusion.28 = f32[8,128,128]{2,1,0:T(8,128)} fusion(f32[8,128,128]{2,1,0:T(8,128)S(1)} %bitcast_add_fusion.2, f32[8,128,512]{2,0,1:T(8,128)} %fusion, f32[8,128,512]{2,0,1:T(8,128)S(1)} %fusion.2, pred[8]{0:T(512)(128)(4,1)S(1)} %get-tuple-element.31), kind=kOutput, calls=%fused_computation.42 | convolution fusion | flops 805568512 | bytes 5242888 | tf_op jit(solution)/shard_map/sra,sca->src/dot_general | solution.py:233
  (166 shorter events, 120.2 us)
Async XLA Ops:
  7.2 130.3 %copy-start = (f32[32,128]{1,0:T(8,128)S(1)}, f32[32,128]{1,0:T(8,128)}, u32[]{:S(2)}) copy-start(f32[32,128]{1,0:T(8,128)} %param.21) | copy-start | bytes 49156
  11.7 4.1 copy-start.19
  18.4 3.5 copy-start.11
  41.2 4.4 copy-start.13
  41.2 5.1 copy-start.17
  41.2 5.1 copy-start.18
  41.2 32.9 %copy-start.12 = (f32[60,144,1]{1,0,2:T(8,128)S(1)}, f32[60,144,1]{1,0,2:T(8,128)}, u32[]{:S(2)}) copy-start(f32[60,144,1]{1,0,2:T(8,128)} %constant.428) | copy-start | bytes 103684
  41.2 32.9 %all-to-all-start = ((f32[4,36,32,128]{3,2,1,0:T(8,128)}), f32[4,36,32,128]{3,2,1,0:T(8,128)S(1)}, u32[]{:S(2)}, u32[]{:S(2)}) async-start(f32[4,36,32,128]{3,2,1,0:T(8,128)} %pad_maximum_fusion.1), calls=%async_computation | async-start | bytes 4718592 | tf_op jit(solution)/shard_map/all_to_all | solution.py:130
  79.1 51.6 %all-to-all-start.1 = ((f32[88,32,128]{2,1,0:T(8,128)}), f32[88,32,128]{2,1,0:T(8,128)S(1)}, u32[]{:S(2)}, u32[]{:S(2)}) async-start(f32[88,32,128]{2,1,0:T(8,128)} %copy.81), calls=%async_computation.1 | async-start | bytes 2883584 | tf_op jit(solution)/shard_map/all_to_all | solution.py:154
  133.2 12.3 %all-to-all-start.2 = ((f32[32,32,128]{2,1,0:T(8,128)}), f32[32,32,128]{2,1,0:T(8,128)S(1)}, u32[]{:S(2)}, u32[]{:S(2)}) async-start(f32[32,32,128]{2,1,0:T(8,128)} %copy.83), calls=%async_computation.2 | async-start | bytes 1048576 | tf_op jit(solution)/shard_map/all_to_all | solution.py:165
  136.7 155.9 %all-reduce.4.cloned.1.call-start = ((), (), s32[]{:S(2)}) async-start(), calls=%async_computation.3 | async-start | bytes 7864320 | tf_op jit(solution)/shard_map/psum | solution.py:200
  153.0 7.8 %copy-start.16 = (s32[72]{0:T(128)S(1)}, s32[72]{0:T(128)}, u32[]{:S(2)}) copy-start(s32[72]{0:T(128)} %constant.427) | copy-start | bytes 868
  153.0 18.1 %copy-start.15 = (f32[1,128]{1,0:T(1,128)S(1)}, f32[1,128]{1,0:T(1,128)}, u32[]{:S(2)}) copy-start(f32[1,128]{1,0:T(1,128)} %param.20) | copy-start | bytes 1540
  158.0 6.7 %collective-permute-start = (f32[128]{0:T(128)S(1)}, f32[128]{0:T(128)S(1)}, u32[]{:S(2)}, u32[]{:S(2)}) collective-permute-start(f32[128]{0:T(128)S(1)} %get-tuple-element.64), channel_id=1, source_target_pairs={{0,1},{1,2},{2,3},{3,4},{4,5},{5,6},{6,7},{7,8},{8,9},{9,10},{10,1... | collective-permute-start | bytes 1544 | tf_op jit(solution)/shard_map/ppermute | solution.py:16
  158.1 7.2 %collective-permute-start.1 = (f32[128]{0:T(128)S(1)}, f32[128]{0:T(128)S(1)}, u32[]{:S(2)}, u32[]{:S(2)}) collective-permute-start(f32[128]{0:T(128)S(1)} %get-tuple-element.70), channel_id=1, source_target_pairs={{0,2},{1,3},{2,4},{3,5},{4,6},{5,7},{6,8},{7,9},{8,10},{9,11},{10,... | collective-permute-start | bytes 1544 | tf_op jit(solution)/shard_map/ppermute | solution.py:16
  158.5 8.8 %collective-permute-start.2 = (f32[128]{0:T(128)S(1)}, f32[128]{0:T(128)S(1)}, u32[]{:S(2)}, u32[]{:S(2)}) collective-permute-start(f32[128]{0:T(128)S(1)} %get-tuple-element.69), channel_id=1, source_target_pairs={{0,3},{1,4},{2,5},{3,6},{4,7},{5,8},{6,9},{7,10},{8,11},{9,12},{10... | collective-permute-start | bytes 1544 | tf_op jit(solution)/shard_map/ppermute | solution.py:16
  160.8 6.5 %collective-permute-start.3 = (f32[128]{0:T(128)S(1)}, f32[128]{0:T(128)S(1)}, u32[]{:S(2)}, u32[]{:S(2)}) collective-permute-start(f32[128]{0:T(128)S(1)} %get-tuple-element.68), channel_id=1, source_target_pairs={{0,4},{1,5},{2,6},{3,7},{4,8},{5,9},{6,10},{7,11},{8,12},{9,13},{1... | collective-permute-start | bytes 1544 | tf_op jit(solution)/shard_map/ppermute | solution.py:16
  160.8 6.5 %collective-permute-start.4 = (f32[128]{0:T(128)S(1)}, f32[128]{0:T(128)S(1)}, u32[]{:S(2)}, u32[]{:S(2)}) collective-permute-start(f32[128]{0:T(128)S(1)} %get-tuple-element.67), channel_id=1, source_target_pairs={{0,5},{1,6},{2,7},{3,8},{4,9},{5,10},{6,11},{7,12},{8,13},{9,14},{... | collective-permute-start | bytes 1544 | tf_op jit(solution)/shard_map/ppermute | solution.py:16
  164.8 6.3 %collective-permute-start.5 = (f32[128]{0:T(128)S(1)}, f32[128]{0:T(128)S(1)}, u32[]{:S(2)}, u32[]{:S(2)}) collective-permute-start(f32[128]{0:T(128)S(1)} %get-tuple-element.66), channel_id=1, source_target_pairs={{0,6},{1,7},{2,8},{3,9},{4,10},{5,11},{6,12},{7,13},{8,14},{9,15},... | collective-permute-start | bytes 1544 | tf_op jit(solution)/shard_map/ppermute | solution.py:16
  165.3 5.7 %collective-permute-start.6 = (f32[128]{0:T(128)S(1)}, f32[128]{0:T(128)S(1)}, u32[]{:S(2)}, u32[]{:S(2)}) collective-permute-start(f32[128]{0:T(128)S(1)} %get-tuple-element.65), channel_id=1, source_target_pairs={{0,7},{1,8},{2,9},{3,10},{4,11},{5,12},{6,13},{7,14},{8,15},{9,16}... | collective-permute-start | bytes 1544 | tf_op jit(solution)/shard_map/ppermute | solution.py:16
  319.7 16.6 %copy-start.10 = (f32[512,512]{1,0:T(8,128)S(1)}, f32[512,512]{1,0:T(8,128)}, u32[]{:S(2)}) copy-start(f32[512,512]{1,0:T(8,128)} %copy-done.9) | copy-start | bytes 3145732
  406.5 49.4 %copy-start.8 = (f32[512,512]{1,0:T(8,128)}, f32[512,512]{1,0:T(8,128)S(1)}, u32[]{:S(2)}) copy-start(f32[512,512]{1,0:T(8,128)S(1)} %get-tuple-element.140) | copy-start | bytes 3145732
  469.6 7.7 %copy-start.2 = (f32[2304,512]{1,0:T(8,128)S(1)}, f32[2304,512]{1,0:T(8,128)}, u32[]{:S(2)}) copy-start(f32[2304,512]{1,0:T(8,128)} %copy.92) | copy-start | bytes 14155780
  492.4 8.5 %copy-start.1 = (f32[32,128]{1,0:T(8,128)S(1)}, f32[32,128]{1,0:T(8,128)}, u32[]{:S(2)}) copy-start(f32[32,128]{1,0:T(8,128)} %param.21) | copy-start | bytes 49156
  (7 other events, 11.4 us)
Sparse Core Ops, SparseCore 0:
  153.1 139.4 all-reduce.3
